TPU v7x, 32 devices: a whole 2x2x4 slice. The times are simulated.
32 devices in a mesh: groups: 2 (over x), branch: 4 (over y, core), head: 4 (over z).
Axes of the slice: x: 2, y: 2, z: 4, core: 2. Of those that a mesh axis runs over, the one named last changes fastest.
Arguments:
- queries: bfloat16 [128, 8192], P(('groups', 'branch'), 'head'), parts along dimension 0, may hold values from -100 to 100, as said below
- root_keys: bfloat16 [32768, 1024], P(('groups', 'branch'), 'head'), parts along dimension 0, may hold values from -6 to 6
- root_values: bfloat16 [32768, 1024], P(('groups', 'branch'), 'head'), parts along dimension 0, may hold values from -6 to 6
- branch_keys: bfloat16 [8, 4096, 1024], P(('groups', 'branch'), None, 'head'), parts along dimension 0, may hold values from -6 to 6
- branch_values: bfloat16 [8, 4096, 1024], P(('groups', 'branch'), None, 'head'), parts along dimension 0, may hold values from -6 to 6
- branch_lengths: int32 [8], P(('groups', 'branch')), parts along dimension 0, may hold values from 512 to 4096, as said below
- row_branch: int32 [128], P('groups'), parts along dimension 0, may hold values from 0 to 3, as said below
Outputs:
- attended: bfloat16 [128, 8192], P(('groups', 'branch'), 'head'), parts along dimension 0
There are 2 independent parts, one for each index of `groups`. A program takes and returns all parts, laid end to end along the dimension named above; each array names one. Nothing has to cross between parts.
Inputs may be any that keep to these rules, and one draw needn't show every extreme that they name: `queries`: query entries; rows may differ in scale. `row_branch`: no branch has more than 32 rows; some branch has exactly 32. `branch_lengths`: some branch has exactly 4096 live tokens.
All inputs are finite; a program needn't handle non-finite values.
Results may differ from a plain program's by a relative error of at most 0.006.
Values may be sent and summed in bfloat16 or wider, within the bound.
A program may use at most 128 MiB of HBM per device.

v0:
```python
import jax
import jax.numpy as jnp
from jax import lax
from jax.sharding import PartitionSpec as P

QHEADS = 64
KVHEADS = 8
HD = 128


NEG = -1e30


def combined_all(value, axis, join):
    pieces = jax.tree.map(lambda part: lax.all_gather(part, axis), value)
    head = jax.tree.map(lambda part: part[0], pieces)
    tail = jax.tree.map(lambda part: part[1:], pieces)
    running, _ = lax.scan(lambda running, piece: (join(running, piece), None), head, tail)
    return running


def empty_part(count, width, head_dim):
    return (
        jnp.full((count, width), NEG, jnp.float32),
        jnp.zeros((count, width), jnp.float32),
        jnp.zeros((count, width, head_dim), jnp.float32),
    )


def combine(first, second):
    peak = jnp.maximum(first[0], second[0])
    scale_a = jnp.exp(first[0] - peak)
    scale_b = jnp.exp(second[0] - peak)
    return (
        peak,
        first[1] * scale_a + second[1] * scale_b,
        first[2] * scale_a[..., None] + second[2] * scale_b[..., None],
    )


def attend_block(query, keys, values, valid, factor):
    count, groups, per_group, head_dim = query.shape
    scores = jnp.einsum("rgph,bgh->rgpb", query, keys, preferred_element_type=jnp.float32) * factor
    scores = jnp.where(valid, scores, NEG)
    peak = jnp.max(scores, axis=-1)
    weights = jnp.where(valid, jnp.exp(scores - peak[..., None]), 0.0)
    total = jnp.sum(weights, axis=-1)
    mixed = jnp.einsum(
        "rgpb,bgh->rgph", weights.astype(jnp.bfloat16), values, preferred_element_type=jnp.float32
    )
    width = groups * per_group
    return (
        peak.reshape(count, width),
        total.reshape(count, width),
        mixed.reshape(count, width, head_dim),
    )


def on_device(
    queries, root_keys, root_values, branch_keys, branch_values, branch_lengths, row_branch
):
    head_dim = HD
    per_group = QHEADS // KVHEADS
    local_rows = queries.shape[0]
    all_rows = row_branch.shape[0]
    groups = root_keys.shape[1] // head_dim
    width = groups * per_group
    slots_count = 2 * local_rows
    factor = head_dim ** (-0.5)
    branch_id = lax.axis_index("branch")
    member = row_branch == branch_id
    ranking = jnp.cumsum(member.astype(jnp.int32)) - 1
    picker = member[None, :] & (
        ranking[None, :] == jnp.arange(slots_count, dtype=jnp.int32)[:, None]
    )
    picker_half = picker.astype(jnp.bfloat16)
    root_block = min(512, root_keys.shape[0])
    root_k = root_keys.reshape(root_keys.shape[0] // root_block, root_block, groups, head_dim)
    root_v = root_values.reshape(root_values.shape[0] // root_block, root_block, groups, head_dim)
    all_valid = jnp.ones((root_block,), dtype=bool)
    piece = lax.all_gather(queries, "branch", axis=0, tiled=True)
    count = piece.shape[0]
    query = piece.reshape(count, groups, per_group, head_dim)

    def one_block(state, pair):
        return (combine(state, attend_block(query, pair[0], pair[1], all_valid, factor)), None)

    part, _ = lax.scan(one_block, empty_part(count, width, head_dim), (root_k, root_v))
    peak_all = part[0]
    total_all = part[1]
    mixed_all = part[2]
    chosen = jnp.dot(picker_half, piece, preferred_element_type=jnp.float32)
    root_peak, root_total, root_mixed, chosen = (peak_all, total_all, mixed_all, chosen)
    branch_query = chosen.astype(jnp.bfloat16).reshape(slots_count, groups, per_group, head_dim)
    length = branch_lengths[0]
    keys_here = branch_keys[0]
    values_here = branch_values[0]
    block = min(512, keys_here.shape[0])
    blocks_used = (length + block - 1) // block

    def branch_step(index, state):
        offset = index * block
        keys_block = lax.dynamic_slice_in_dim(keys_here, offset, block, 0).reshape(
            block, groups, head_dim
        )
        values_block = lax.dynamic_slice_in_dim(values_here, offset, block, 0).reshape(
            block, groups, head_dim
        )
        valid = offset + jnp.arange(block, dtype=jnp.int32) < length
        return combine(state, attend_block(branch_query, keys_block, values_block, valid, factor))

    branch_part = lax.fori_loop(
        0, blocks_used, branch_step, empty_part(slots_count, width, head_dim)
    )
    picker_full = picker.astype(jnp.float32)
    spread_peak = jnp.max(jnp.where(picker[:, :, None], branch_part[0][:, None, :], NEG), axis=0)
    spread_total = jnp.einsum(
        "sr,sk->rk", picker_full, branch_part[1], precision=lax.Precision.HIGHEST
    )
    spread_mixed = jnp.einsum(
        "sr,sk->rk",
        picker_full,
        branch_part[2].reshape(slots_count, width * head_dim),
        precision=lax.Precision.HIGHEST,
    )
    peak, total, mixed = combine(
        (root_peak, root_total, root_mixed),
        (spread_peak, spread_total, spread_mixed.reshape(all_rows, width, head_dim)),
    )
    merged = combined_all((peak, total, mixed), "branch", combine)
    first_row = branch_id * local_rows
    own_total = lax.dynamic_slice_in_dim(merged[1], first_row, local_rows, 0)
    own_mixed = lax.dynamic_slice_in_dim(merged[2], first_row, local_rows, 0)
    finished = own_mixed / own_total[..., None]
    return finished.reshape(local_rows, width * head_dim).astype(jnp.bfloat16)


def solution(mesh):
    placed = (
        P(("groups", "branch"), "head"),
        P(("groups", "branch"), "head"),
        P(("groups", "branch"), "head"),
        P(("groups", "branch"), None, "head"),
        P(("groups", "branch"), None, "head"),
        P(("groups", "branch")),
        P("groups"),
    )
    return jax.shard_map(
        on_device,
        mesh=mesh,
        in_specs=placed,
        out_specs=P(("groups", "branch"), "head"),
        check_vma=False,
    )
```

profile of v0, /device:TPU:0, one launch (start us, length us, event | category | flops | bytes accessed | tf_op | source)
XLA Modules:
  0.0 120.1 jit_solution(15412547363303058967)
XLA Ops:
  7.2 4.1 %reshape.151 = bf16[8,512,2,128]{3,2,1,0:T(2,128)(2,1)} reshape(bf16[4096,256]{1,0:T(8,128)(2,1)} %param.14) | data formatting | bytes 4194304 | tf_op jit(solution)/shard_map/reshape | solution.py:78
  11.4 7.2 %all_gather.21 = bf16[64,2048]{1,0:T(8,128)(2,1)S(1)} all-gather(bf16[16,2048]{1,0:T(8,128)(2,1)S(1)} %copy-done.1), channel_id=1, replica_groups=mesh['groups'=2,'branch'=4,'head'=4] {'branch'}, dimensions={0}, use_global_device_ids=true | all-gather | bytes 327680 | tf_op jit(solution)/shard_map/all_gather | solution.py:81
  19.2 2.1 %reshape.152 = bf16[8,512,2,128]{3,2,1,0:T(2,128)(2,1)} reshape(bf16[4096,256]{1,0:T(8,128)(2,1)S(1)} %copy-done) | data formatting | bytes 4194304 | tf_op jit(solution)/shard_map/reshape | solution.py:79
  21.3 28.8 %while.45 = (s32[]{:T(128)}, f32[64,16]{0,1:T(8,128)S(1)}, f32[64,16]{0,1:T(8,128)S(1)}, f32[64,16,128]{2,0,1:T(8,128)S(1)}, bf16[8,512,2,128]{3,2,1,0:T(2,128)(...) while((s32[]{:T(128)}, f32[64,16]{0,1:T(8,128)S(1)}, ...), condition=%wide.region_3.4_spmd.clone, body=%wide.region_0.3_spmd.clone.sunk | while | flops 273160192 | bytes 10281076 | solution.py:88
  21.3 1.4 %constant_dynamic-slice_fusion.11 = (bf16[1,512,2,128]{3,2,1,0:T(2,128)(2,1)S(1)}, bf16[1,512,2,128]{3,2,1,0:T(2,128)(2,1)S(1)}) fusion(bf16[8,512,2,128]{3,2,1,0:T(2,128)(2,1)} %get-tuple-element.526, s32[]{:T(128)S(6)} %copy.127, bf16[8,512,2,128]{3,2,1,0:T(2,128)(2,1)} %get-tuple-element.524), kind=kLoop, calls=%fused_computation.53.clone.1 | loop fusion | bytes 1048580 | tf_op jit(solution)/shard_map/while/body/jit(dynamic_index_in_dim)/dynamic_slice | solution.py:88
  22.7 0.5 bitcast_reduce_fusion.2
  23.2 0.6 fusion.83
  23.8 0.5 fusion.85
  24.4 0.5 fusion.86
  24.9 1.4 %constant_dynamic-slice_fusion.11 = (bf16[1,512,2,128]{3,2,1,0:T(2,128)(2,1)S(1)}, bf16[1,512,2,128]{3,2,1,0:T(2,128)(2,1)S(1)}) fusion(bf16[8,512,2,128]{3,2,1,0:T(2,128)(2,1)} %get-tuple-element.526, s32[]{:T(128)S(6)} %copy.127, bf16[8,512,2,128]{3,2,1,0:T(2,128)(2,1)} %get-tuple-element.524), kind=kLoop, calls=%fused_computation.53.clone.1 | loop fusion | bytes 1048580 | tf_op jit(solution)/shard_map/while/body/jit(dynamic_index_in_dim)/dynamic_slice | solution.py:88
  26.3 0.5 bitcast_reduce_fusion.2
  26.8 0.6 fusion.83
  27.4 0.5 fusion.85
  27.9 0.5 fusion.86
  28.5 1.4 %constant_dynamic-slice_fusion.11 = (bf16[1,512,2,128]{3,2,1,0:T(2,128)(2,1)S(1)}, bf16[1,512,2,128]{3,2,1,0:T(2,128)(2,1)S(1)}) fusion(bf16[8,512,2,128]{3,2,1,0:T(2,128)(2,1)} %get-tuple-element.526, s32[]{:T(128)S(6)} %copy.127, bf16[8,512,2,128]{3,2,1,0:T(2,128)(2,1)} %get-tuple-element.524), kind=kLoop, calls=%fused_computation.53.clone.1 | loop fusion | bytes 1048580 | tf_op jit(solution)/shard_map/while/body/jit(dynamic_index_in_dim)/dynamic_slice | solution.py:88
  29.9 0.5 bitcast_reduce_fusion.2
  30.4 0.6 fusion.83
  31.0 0.5 fusion.85
  31.5 0.5 fusion.86
  32.1 1.4 %constant_dynamic-slice_fusion.11 = (bf16[1,512,2,128]{3,2,1,0:T(2,128)(2,1)S(1)}, bf16[1,512,2,128]{3,2,1,0:T(2,128)(2,1)S(1)}) fusion(bf16[8,512,2,128]{3,2,1,0:T(2,128)(2,1)} %get-tuple-element.526, s32[]{:T(128)S(6)} %copy.127, bf16[8,512,2,128]{3,2,1,0:T(2,128)(2,1)} %get-tuple-element.524), kind=kLoop, calls=%fused_computation.53.clone.1 | loop fusion | bytes 1048580 | tf_op jit(solution)/shard_map/while/body/jit(dynamic_index_in_dim)/dynamic_slice | solution.py:88
  33.5 0.5 bitcast_reduce_fusion.2
  34.0 0.6 fusion.83
  34.6 0.5 fusion.85
  35.1 0.5 fusion.86
  35.7 1.4 %constant_dynamic-slice_fusion.11 = (bf16[1,512,2,128]{3,2,1,0:T(2,128)(2,1)S(1)}, bf16[1,512,2,128]{3,2,1,0:T(2,128)(2,1)S(1)}) fusion(bf16[8,512,2,128]{3,2,1,0:T(2,128)(2,1)} %get-tuple-element.526, s32[]{:T(128)S(6)} %copy.127, bf16[8,512,2,128]{3,2,1,0:T(2,128)(2,1)} %get-tuple-element.524), kind=kLoop, calls=%fused_computation.53.clone.1 | loop fusion | bytes 1048580 | tf_op jit(solution)/shard_map/while/body/jit(dynamic_index_in_dim)/dynamic_slice | solution.py:88
  37.1 0.5 bitcast_reduce_fusion.2
  37.6 0.6 fusion.83
  38.2 0.5 fusion.85
  38.7 0.5 fusion.86
  39.3 1.4 %constant_dynamic-slice_fusion.11 = (bf16[1,512,2,128]{3,2,1,0:T(2,128)(2,1)S(1)}, bf16[1,512,2,128]{3,2,1,0:T(2,128)(2,1)S(1)}) fusion(bf16[8,512,2,128]{3,2,1,0:T(2,128)(2,1)} %get-tuple-element.526, s32[]{:T(128)S(6)} %copy.127, bf16[8,512,2,128]{3,2,1,0:T(2,128)(2,1)} %get-tuple-element.524), kind=kLoop, calls=%fused_computation.53.clone.1 | loop fusion | bytes 1048580 | tf_op jit(solution)/shard_map/while/body/jit(dynamic_index_in_dim)/dynamic_slice | solution.py:88
  40.7 0.5 bitcast_reduce_fusion.2
  41.2 0.6 fusion.83
  41.8 0.5 fusion.85
  42.3 0.5 fusion.86
  42.9 1.4 %constant_dynamic-slice_fusion.11 = (bf16[1,512,2,128]{3,2,1,0:T(2,128)(2,1)S(1)}, bf16[1,512,2,128]{3,2,1,0:T(2,128)(2,1)S(1)}) fusion(bf16[8,512,2,128]{3,2,1,0:T(2,128)(2,1)} %get-tuple-element.526, s32[]{:T(128)S(6)} %copy.127, bf16[8,512,2,128]{3,2,1,0:T(2,128)(2,1)} %get-tuple-element.524), kind=kLoop, calls=%fused_computation.53.clone.1 | loop fusion | bytes 1048580 | tf_op jit(solution)/shard_map/while/body/jit(dynamic_index_in_dim)/dynamic_slice | solution.py:88
  44.3 0.5 bitcast_reduce_fusion.2
  44.8 0.6 fusion.83
  45.4 0.5 fusion.85
  45.9 0.5 fusion.86
  46.5 1.4 %constant_dynamic-slice_fusion.11 = (bf16[1,512,2,128]{3,2,1,0:T(2,128)(2,1)S(1)}, bf16[1,512,2,128]{3,2,1,0:T(2,128)(2,1)S(1)}) fusion(bf16[8,512,2,128]{3,2,1,0:T(2,128)(2,1)} %get-tuple-element.526, s32[]{:T(128)S(6)} %copy.127, bf16[8,512,2,128]{3,2,1,0:T(2,128)(2,1)} %get-tuple-element.524), kind=kLoop, calls=%fused_computation.53.clone.1 | loop fusion | bytes 1048580 | tf_op jit(solution)/shard_map/while/body/jit(dynamic_index_in_dim)/dynamic_slice | solution.py:88
  48.4 0.6 fusion.83
  49.5 0.5 fusion.86
  50.1 2.9 %copy.64 = bf16[1,4096,256]{1,2,0:T(8,128)(2,1)S(1)} copy(bf16[1,4096,256]{2,1,0:T(8,128)(2,1)} %param.16) | data formatting | bytes 4194304 | tf_op args[3]
  53.1 4.1 %copy.65 = bf16[1,4096,256]{1,2,0:T(8,128)(2,1)} copy(bf16[1,4096,256]{2,1,0:T(8,128)(2,1)} %param.17) | data formatting | bytes 4194304 | tf_op args[4]
  57.2 12.3 %while.43 = (s32[]{:T(128)}, f32[32,16]{0,1:T(8,128)S(1)}, f32[32,16]{0,1:T(8,128)S(1)}, f32[32,16,128]{2,0,1:T(8,128)S(1)}, s32[]{:T(128)}, /*index=5*/s32[]{:T...) while((s32[]{:T(128)}, f32[32,16]{0,1:T(8,128)S(1)}, ...), condition=%wide.region_8.9_spmd, body=%wide.region_5.8_spmd.sunk | while | flops 136776704 | bytes 5929151 | solution.py:112
  57.3 1.0 constant_dynamic-slice_fusion.9
  58.3 0.7 add_compare_fusion.2
  60.3 1.0 constant_dynamic-slice_fusion.9
  61.3 0.7 add_compare_fusion.2
  63.4 1.0 constant_dynamic-slice_fusion.9
  64.4 0.7 add_compare_fusion.2
  66.5 1.0 constant_dynamic-slice_fusion.9
  67.5 0.7 add_compare_fusion.2
  69.8 1.3 %fusion.29 = f32[64,16,128]{2,0,1:T(8,128)} fusion(f32[64,16,128]{2,0,1:T(8,128)S(1)} %get-tuple-element.136, f32[64,16]{0,1:T(8,128)S(1)} %get-tuple-element.318, f32[64,16]{0,1:T(8,128)S(1)} %get-tuple-element.317, s32[64]{0:T(128)S(1)} %add_reduce_fusion, pred[64]{0:T(512)(128)(4,1)S(1)} %get-tuple-element.308, f32[32,16,128]{2,0,1:T(8,128)S(1)} %get-tuple-element.137), kind=kOutput, calls=%fused_computation.58 | convolution fusion | flops 50728960 | bytes 1319232 | tf_op jit(solution)/shard_map/sr,sk->rk/dot_general | solution.py:120
  71.1 16.5 %all-gather.3 = f32[4,64,16]{1,2,0:T(8,128)S(1)} all-gather(f32[1,64,16]{1,2,0:T(8,128)S(1)} %get-tuple-element.319), channel_id=2, replica_groups=mesh['groups'=2,'branch'=4,'head'=4] {'branch'}, dimensions={0}, use_global_device_ids=true | all-gather | bytes 20480 | tf_op jit(solution)/shard_map/all_gather | solution.py:15
  87.7 5.2 %all-gather.4 = f32[4,64,16]{1,2,0:T(8,128)S(1)} all-gather(f32[1,64,16]{1,2,0:T(8,128)S(1)} %fusion.32), channel_id=3, replica_groups=mesh['groups'=2,'branch'=4,'head'=4] {'branch'}, dimensions={0}, use_global_device_ids=true | all-gather | bytes 20480 | tf_op jit(solution)/shard_map/all_gather | solution.py:15
  92.9 14.4 %all-gather.7.cloned.1.call-done = f32[256,16,128]{2,0,1:T(8,128)} async-done(((f32[64,16,128]{2,0,1:T(8,128)}), f32[256,16,128]{2,0,1:T(8,128)}) %all-gather.7.cloned.1.call-update) | async-done | bytes 2097168 | tf_op jit(solution)/shard_map/all_gather | solution.py:15
  107.3 1.1 slice.36
  108.8 1.1 slice-done
  109.8 2.5 %while.44 = (s32[]{:T(128)}, f32[64,16]{0,1:T(8,128)S(1)}, f32[64,16]{0,1:T(8,128)S(1)}, f32[64,16,128]{2,1,0:T(8,128)S(1)}, f32[3,64,16]{1,2,0:T(8,128)S(1)}, /...) while((s32[]{:T(128)}, f32[64,16]{0,1:T(8,128)S(1)}, f32[64,16]{0,1:T(8,128)S(1)}, ...), condition=%wide.region_11.12_spmd, body=%wide.region_10.11_spmd.sunk | while | flops 399362 | bytes 2678885 | solution.py:18
  110.1 0.6 fusion.80
  110.9 0.6 fusion.80
  111.8 0.6 fusion.80
  112.6 0.6 copy.112
  (79 shorter events, 9.0 us)
Async XLA Ops:
  6.5 100.8 %all-gather.7.cloned.1.call-start = ((), (), s32[]{:S(2)}) async-start(), calls=%async_computation | async-start | bytes 2621440 | tf_op jit(solution)/shard_map/all_gather | solution.py:15
  7.2 4.2 %copy-start.1 = (bf16[16,2048]{1,0:T(8,128)(2,1)S(1)}, bf16[16,2048]{1,0:T(8,128)(2,1)}, u32[]{:S(2)}) copy-start(bf16[16,2048]{1,0:T(8,128)(2,1)} %param.13) | copy-start | bytes 196612
  7.2 11.4 %copy-start.2 = (s32[64]{0:T(128)S(1)}, s32[64]{0:T(128)}, u32[]{:S(2)}) copy-start(s32[64]{0:T(128)} %param.19) | copy-start | bytes 772
  7.2 12.0 %copy-start = (bf16[4096,256]{1,0:T(8,128)(2,1)S(1)}, bf16[4096,256]{1,0:T(8,128)(2,1)}, u32[]{:S(2)}) copy-start(bf16[4096,256]{1,0:T(8,128)(2,1)} %param.15) | copy-start | bytes 6291460
  108.4 1.4 %slice-start = ((f32[256,16,128]{2,0,1:T(8,128)}), f32[192,16,128]{2,0,1:T(8,128)S(1)}, s32[]{:S(2)}) async-start(f32[256,16,128]{2,0,1:T(8,128)} %all-gather.7.cloned.1.call-done), calls=%async_computation.1 | async-start | bytes 3145728 | tf_op jit(solution)/shard_map/slice | solution.py:17
Sparse Core Ops, SparseCore 0:
  71.2 36.1 all-gather.6
where the time goes:
time: 121 us; the launch traced here: 120 us
  local copies, waits for them, and re-layouts  32.7 us (27%)
  blocking collectives  28.9 us (24%)
  other arithmetic  16.3 us (13%)
  waiting for transfers between devices  14.5 us (12%)
  between operations  14.2 us (12%)
  matrix products  12.8 us (11%)
    all_gather x2, blocking collectives, combined_all(): pieces = jax.tree.map(lambda part: lax.all_gather(part, axis), value)  21.7 us
    all_gather x1, waiting for transfers between devices, combined_all(): pieces = jax.tree.map(lambda part: lax.all_gather(part, axis), value)  14.4 us
    dynamic_slice x8, local copies, waits for them, and re-layouts, on_device(): lax.scan(one_block, empty_part(count, width, head_dim), (root_k, root_v))  11.2 us
    unnamed x12, local copies, waits for them, and re-layouts  7.84 us
    all_gather x1, blocking collectives, on_device(): piece = lax.all_gather(queries, 'branch', axis=0, tiled=True)  7.24 us
    add x15, other arithmetic, combine(): first[2] * scale_a[..., None] + second[2] * scale_b[..., None]  6.95 us
    reduce_sum x12, other arithmetic, attend_block(): total = jnp.sum(weights, axis=-1)  6 us
    dot_general x12, matrix products, attend_block(): jnp.einsum('rgpb,bgh->rgph', weights.astype(jnp.bfloat16), values, prefer...  5.68 us
  transfers between devices with their start and end apart: 1, of which 1 were waited for; matrix products, arithmetic and copies ran while one was open for 0% of the time, Pallas kernels for 0%

commit v1 on v0

v1 whole, which is shorter than its diff:
```python
import functools
import math

import jax
import jax.numpy as jnp
from jax import lax
from jax.experimental import pallas as pl
from jax.experimental.pallas import tpu as pltpu
from jax.sharding import PartitionSpec as P

HD = 128
PER = 8
NEG = -1e30
MESH = pl.DeviceIdType.MESH
BF = jnp.bfloat16
F32 = jnp.float32


def split(value, parts):
    pieces = []
    for _ in range(parts):
        piece = value.astype(BF)
        pieces.append(piece)
        value = value - piece.astype(F32)
    return pieces


def kernel(
    n, rows, tokens, groups, tb,
    q_ref, rb_ref, len_ref, rk_ref, rv_ref, bk_ref, bv_ref, out_ref,
    qall, kbuf, vbuf, qbr, sbuf, mbuf, acc, rnum, rm, spread_e,
    send_o, send_l, recv_o, recv_l,
    kv_sem, q_own, q_send, q_recv, o_send, o_recv, l_send, l_recv,
):
    me = lax.axis_index("branch")
    slots = 2 * rows
    m_rows = slots * PER
    chunks = n // 2
    all_rows = n * rows
    part = rows * PER
    blocks = tokens // tb
    factor = math.log2(math.e) / math.sqrt(HD)

    copies = [
        pltpu.make_async_copy(src, dst, kv_sem.at[i])
        for i, (src, dst) in enumerate((
            (rk_ref, kbuf.at[0]), (rv_ref, vbuf.at[0]),
            (bk_ref.at[0], kbuf.at[1]), (bv_ref.at[0], vbuf.at[1]),
        ))
    ]
    own = pltpu.make_async_copy(q_ref, qall.at[me], q_own)
    own.start()
    for copy in copies:
        copy.start()

    barrier = pltpu.get_barrier_semaphore()
    for off in range(1, n):
        peer = me ^ off
        pl.semaphore_signal(barrier, inc=1, device_id={"branch": peer}, device_id_type=MESH)
    pl.semaphore_wait(barrier, n - 1)

    q_copies = []
    for off in range(1, n):
        peer = me ^ off
        copy = pltpu.make_async_remote_copy(
            src_ref=q_ref, dst_ref=qall.at[me], send_sem=q_send.at[off],
            recv_sem=q_recv.at[off], device_id={"branch": peer}, device_id_type=MESH,
        )
        copy.start()
        q_copies.append(copy)

    rb = rb_ref[...]
    mem_row = jnp.where(rb == me, 1.0, 0.0).astype(F32)
    r_sub = lax.broadcasted_iota(jnp.int32, (all_rows, all_rows), 0)
    r_lane = lax.broadcasted_iota(jnp.int32, (all_rows, all_rows), 1)
    mem_b = jnp.broadcast_to(mem_row, (all_rows, all_rows))
    mem_col = jnp.sum(jnp.where(r_sub == r_lane, mem_b, 0.0), axis=1, keepdims=True)
    rank_col = jnp.sum(jnp.where(r_lane < r_sub, mem_b, 0.0), axis=1, keepdims=True)
    mem_cb = jnp.broadcast_to(mem_col, (all_rows, all_rows))
    rank_row = jnp.sum(jnp.where(r_sub < r_lane, mem_cb, 0.0), axis=0, keepdims=True)
    slot_sub = lax.broadcasted_iota(jnp.int32, (slots, all_rows), 0).astype(F32)
    picker = jnp.where(
        (jnp.broadcast_to(rank_row, (slots, all_rows)) == slot_sub)
        & (jnp.broadcast_to(mem_row, (slots, all_rows)) > 0.5), 1.0, 0.0,
    ).astype(BF)
    slot_lane = lax.broadcasted_iota(jnp.int32, (all_rows, slots), 1).astype(F32)
    e_full = jnp.where(
        (jnp.broadcast_to(rank_col, (all_rows, slots)) == slot_lane)
        & (jnp.broadcast_to(mem_col, (all_rows, slots)) > 0.5), 1.0, 0.0,
    ).astype(BF)
    spread_e[...] = e_full
    length = len_ref[0]

    def stack(q, g):
        return jnp.concatenate(
            [q[:, (g * PER + p) * HD:(g * PER + p + 1) * HD] for p in range(PER)], axis=0
        )

    def chunk_of(k):
        return lax.rem(me // 2 + k, chunks)

    tasks = []
    for g in range(groups):
        tasks.append((0, g, 0))
    for g in range(groups):
        for k in range(1, chunks):
            tasks.append((0, g, k))
        tasks.append((1, g, 0))

    waited = set()

    def need(index):
        if index not in waited:
            waited.add(index)
            copies[index].wait()

    def need_q(off):
        key = ("q", off)
        if key not in waited:
            waited.add(key)
            if off == 0:
                own.wait()
            else:
                q_copies[off - 1].wait_recv()

    def stage(first, second, slot):
        if first is not None:
            src, g, k = first
            need(2 * src)
            if src == 0:
                need_q(2 * k)
                need_q(2 * k + 1)
                base = (me // 2) ^ k
                q_here = qall[pl.ds(base * 2, 2)].reshape(slots, groups * PER * HD)
                query = stack(q_here, g)
            else:
                for off in range(n):
                    need_q(off)
                if g == 0:
                    whole = qall[...].reshape(all_rows, groups * PER * HD)
                    qbr[...] = jnp.dot(picker, whole, preferred_element_type=F32).astype(BF)
                query = stack(qbr[...], g)
            mbuf[slot] = jnp.full((m_rows, HD), NEG, F32)
        if second is not None:
            src2, g2, k2 = second
            need(2 * src2 + 1)
            other = 1 - slot
            peak = jnp.max(mbuf[other], axis=1, keepdims=True) * factor
            mbuf[other] = jnp.broadcast_to(peak, (m_rows, HD))
            acc[...] = jnp.zeros_like(acc)

        def body(j, carry):
            start = pl.multiple_of(j * tb, tb)
            if first is not None:
                keys = kbuf[src, pl.ds(start, tb), g * HD:(g + 1) * HD]
                score = lax.dot_general(
                    query, keys, (((1,), (1,)), ((), ())), preferred_element_type=F32
                )
                if src == 1:
                    place = start + lax.broadcasted_iota(jnp.int32, (m_rows, tb), 1)
                    score = jnp.where(place < length, score, NEG)
                top = score[:, :HD]
                for i in range(1, tb // HD):
                    top = jnp.maximum(top, score[:, i * HD:(i + 1) * HD])
                sbuf[slot, j] = score
                mbuf[slot] = jnp.maximum(mbuf[slot], top)
            if second is not None:
                top2 = mbuf[other]
                peaks = jnp.concatenate([top2] * (tb // HD), axis=1)
                weights = jnp.exp2(sbuf[other, j] * factor - peaks).astype(BF)
                values = vbuf[src2, pl.ds(start, tb), g2 * HD:(g2 + 1) * HD]
                wide = jnp.concatenate([values, jnp.ones((tb, HD), BF)], axis=1)
                acc[...] += jnp.dot(weights, wide, preferred_element_type=F32)
            return carry

        lax.fori_loop(0, blocks, body, 0)

        if second is not None and src2 == 0:
            rnum[g2, k2] = acc[...]
            rm[g2, k2] = mbuf[other]

    eye = (
        lax.broadcasted_iota(jnp.int32, (part, part), 0)
        == lax.broadcasted_iota(jnp.int32, (part, part), 1)
    )
    sent = []

    def finish(g, other):
        numer = acc[:, :HD]
        total = acc[:, HD:]
        top = mbuf[other]
        rights = []
        for p in range(PER):
            lo, hi = p * slots, (p + 1) * slots
            a = jnp.concatenate(split(numer[lo:hi], 2) + [jnp.zeros((slots, HD), BF)], axis=0)
            b = jnp.concatenate(split(total[lo:hi], 2) + [jnp.zeros((slots, HD), BF)], axis=0)
            c = jnp.concatenate(split(top[lo:hi], 3), axis=0)
            rights.append(jnp.concatenate([a, b, c], axis=1))
        for k in range(chunks):
            base = (me // 2) ^ k
            e = spread_e[pl.ds(pl.multiple_of(base * slots, slots), slots), :]
            e3 = jnp.concatenate([e, e, e], axis=1)
            has = jnp.sum(e.astype(F32), axis=1, keepdims=True) > 0.5
            has = jnp.broadcast_to(has, (slots, HD))
            whole_o, whole_l = [], []
            for p in range(PER):
                lo, hi = p * slots, (p + 1) * slots
                back = jnp.dot(e3, rights[p], preferred_element_type=F32)
                r_num = rnum[g, k, lo:hi, :HD]
                r_tot = rnum[g, k, lo:hi, HD:]
                r_top = rm[g, k, lo:hi]
                b_top = jnp.where(has, back[:, 2 * HD:], NEG)
                peak = jnp.maximum(r_top, b_top)
                x = jnp.exp2(r_top - peak)
                y = jnp.exp2(b_top - peak)
                num = r_num * x + back[:, :HD] * y
                tot = r_tot * x + back[:, HD:2 * HD] * y
                whole_o.append((num / tot).astype(BF))
                whole_l.append(peak + jnp.log2(tot))
            for half in range(2):
                off_slot = 2 * k + half
                lo, hi = half * rows, (half + 1) * rows
                send_o[g, off_slot] = jnp.concatenate([o[lo:hi] for o in whole_o], axis=0)
                lse = jnp.concatenate([v[lo:hi] for v in whole_l], axis=0)
                line = jnp.sum(jnp.where(eye, lse, 0.0), axis=0, keepdims=True)
                send_l[g, off_slot] = jnp.broadcast_to(line, (8, part))
        for off in range(1, n):
            k = off // 2
            peer = me ^ off
            index = 2 * k + lax.rem(peer, 2)
            pair = []
            for src, dst, s_sem, r_sem in (
                (send_o, recv_o, o_send, o_recv), (send_l, recv_l, l_send, l_recv),
            ):
                copy = pltpu.make_async_remote_copy(
                    src_ref=src.at[g, index], dst_ref=dst.at[g, off],
                    send_sem=s_sem.at[g, off], recv_sem=r_sem.at[g, off],
                    device_id={"branch": peer}, device_id_type=MESH,
                )
                copy.start()
                pair.append(copy)
            sent.append((g, off, pair))

    def collect(g):
        mine = lax.rem(me, 2)
        lines = [send_l[g, mine][:1]]
        outs = [send_o[g, mine]]
        for gg, off, pair in sent:
            if gg == g:
                for copy in pair:
                    copy.wait_recv()
                lines.append(recv_l[g, off][:1])
                outs.append(recv_o[g, off])
        peak = functools.reduce(jnp.maximum, lines)
        scales = [jnp.exp2(line - peak) for line in lines]
        inverse = 1.0 / functools.reduce(jnp.add, scales)
        result = jnp.zeros((part, HD), F32)
        for scale, o in zip(scales, outs):
            diag = jnp.where(eye, jnp.broadcast_to(scale * inverse, (part, part)), 0.0)
            left = jnp.concatenate(split(diag, 2), axis=1)
            result += jnp.dot(left, jnp.concatenate([o, o], axis=0), preferred_element_type=F32)
        result = result.astype(BF)
        for p in range(PER):
            out_ref[:, (g * PER + p) * HD:(g * PER + p + 1) * HD] = result[p * rows:(p + 1) * rows]

    previous = None
    for t, task in enumerate(tasks + [None]):
        stage(task, previous, t % 2)
        if previous is not None and previous[0] == 1:
            finish(previous[1], 1 - t % 2)
        previous = task
    for g in range(groups):
        collect(g)
    for copy in q_copies:
        copy.wait_send()
    for _, _, pair in sent:
        for copy in pair:
            copy.wait_send()


def on_device(
    queries, root_keys, root_values, branch_keys, branch_values, branch_lengths, row_branch
):
    rows = queries.shape[0]
    all_rows = row_branch.shape[0]
    n = all_rows // rows
    tokens, width = root_keys.shape
    groups = width // HD
    chunks = n // 2
    slots = 2 * rows
    m_rows = slots * PER
    part = rows * PER
    tb = min(1024, tokens)
    vmem = pl.BlockSpec(memory_space=pltpu.VMEM)
    smem = pl.BlockSpec(memory_space=pltpu.SMEM)
    hbm = pl.BlockSpec(memory_space=pl.ANY)
    dma = pltpu.SemaphoreType.DMA
    return pl.pallas_call(
        functools.partial(kernel, n, rows, tokens, groups, tb),
        out_shape=jax.ShapeDtypeStruct(queries.shape, BF),
        in_specs=[vmem, vmem, smem, hbm, hbm, hbm, hbm],
        out_specs=vmem,
        scratch_shapes=[
            pltpu.VMEM((n, rows, groups * PER * HD), BF),
            pltpu.VMEM((2, tokens, width), BF),
            pltpu.VMEM((2, tokens, width), BF),
            pltpu.VMEM((slots, groups * PER * HD), BF),
            pltpu.VMEM((2, tokens // tb, m_rows, tb), F32),
            pltpu.VMEM((2, m_rows, HD), F32),
            pltpu.VMEM((m_rows, 2 * HD), F32),
            pltpu.VMEM((groups, chunks, m_rows, 2 * HD), F32),
            pltpu.VMEM((groups, chunks, m_rows, HD), F32),
            pltpu.VMEM((all_rows, slots), BF),
            pltpu.VMEM((groups, n, part, HD), BF),
            pltpu.VMEM((groups, n, 8, part), F32),
            pltpu.VMEM((groups, n, part, HD), BF),
            pltpu.VMEM((groups, n, 8, part), F32),
            dma((4,)), dma, dma((n,)), dma((n,)),
            dma((groups, n)), dma((groups, n)), dma((groups, n)), dma((groups, n)),
        ],
        compiler_params=pltpu.CompilerParams(
            collective_id=0, has_side_effects=True, vmem_limit_bytes=60 * 1024 * 1024
        ),
        name="cascade",
    )(queries, row_branch.reshape(1, all_rows), branch_lengths, root_keys, root_values, branch_keys, branch_values)


def solution(mesh):
    placed = (
        P(("groups", "branch"), "head"),
        P(("groups", "branch"), "head"),
        P(("groups", "branch"), "head"),
        P(("groups", "branch"), None, "head"),
        P(("groups", "branch"), None, "head"),
        P(("groups", "branch")),
        P("groups"),
    )
    return jax.shard_map(
        on_device,
        mesh=mesh,
        in_specs=placed,
        out_specs=P(("groups", "branch"), "head"),
        check_vma=False,
    )
```

time: 121 us -> 25.3 us (0.21)
  local copies, waits for them, and re-layouts: 32.7 us -> 1.47 us
  blocking collectives: 28.9 us -> 0 us
  Pallas kernels: 0 us -> 22.9 us
  other arithmetic: 16.3 us -> 0 us
  waiting for transfers between devices: 14.5 us -> 0 us
  between operations: 14.2 us -> 0.66 us
  matrix products: 12.8 us -> 0 us
    all_gather x3 -> x0, blocking collectives: 28.9 us -> none  [the longest x2 21.7 us: combined_all(): pieces = jax.tree.map(lambda part: lax.all_gather(part, axis), value)]
    pallas_call x0 -> x1, Pallas kernels: none -> 22.9 us  [on_device(): pl.pallas_call(functools.partial(kernel, n, rows, tokens, groups, tb), ou...]
    dynamic_slice x17 -> x0, local copies, waits for them, and re-layouts: 15.4 us -> none  [the longest x8 11.2 us: on_device(): lax.scan(one_block, empty_part(count, width, head_dim), (root_k, root_v))]
    all_gather x1 -> x0, waiting for transfers between devices: 14.4 us -> none  [combined_all(): pieces = jax.tree.map(lambda part: lax.all_gather(part, axis), value)]
    dot_general x27 -> x0, matrix products: 12.8 us -> none  [the longest x12 5.68 us: attend_block(): jnp.einsum('rgpb,bgh->rgph', weights.astype(jnp.bfloat16), values, prefer...]
    add x30 -> x0, other arithmetic: 7.19 us -> none  [the longest x15 6.95 us: combine(): first[2] * scale_a[..., None] + second[2] * scale_b[..., None]]
    unnamed x12 -> x1, local copies, waits for them, and re-layouts: 7.84 us -> 1.47 us
    reshape x2 -> x0, local copies, waits for them, and re-layouts: 6.19 us -> none  [the longest x1 4.12 us: on_device(): root_keys.reshape(root_keys.shape[0] // root_block, root_block, groups, h...]
  transfers between devices with their start and end apart: 1 -> 0, of which waited for: 1 -> 0; matrix products, arithmetic and copies ran while one was open for 0% -> 0% of each run, Pallas kernels for 0% -> 0%
where the time goes in v1:
time: 25.3 us; the launch traced here: 25.1 us
  Pallas kernels  22.9 us (91%)
  local copies, waits for them, and re-layouts  1.47 us (6%)
  between operations  0.66 us (3%)
    pallas_call x1, Pallas kernels, on_device(): pl.pallas_call(functools.partial(kernel, n, rows, tokens, groups, tb), ou...  22.9 us
    unnamed x1, local copies, waits for them, and re-layouts  1.47 us

profile of v1, /device:TPU:0, one launch (start us, length us, event | category | flops | bytes accessed | tf_op | source)
XLA Modules:
  0.0 25.1 jit_solution(1389312339106055243)
XLA Ops:
  0.7 22.9 %cascade.1 = bf16[16,2048]{1,0:T(8,128)(2,1)} custom-call(bf16[16,2048]{1,0:T(8,128)(2,1)} %q_ref.1, s32[1,64]{1,0:T(1,128)} %bitcast.1, s32[1]{0:T(128)S(6)} %copy.9.len_ref, bf16[4096,256]{1,0:T(8,128)(2,1)} %rk_ref.1, bf16[4096,256]{1,0:T(8,128)(2,1)} %rv_ref.1, bf16[1,4096,256]{2,1,0:T(8,128)(2,1)} %bk_ref.1, bf16[1,4096,256]{2,1,0:T(8,128)(2,1)} %bv_ref.1), custom_call_target="tpu_custom_call" | custom-call | tf_op jit(solution)/shard_map/cascade/pallas_call | solution.py:298
  23.6 1.5 %copy.10 = bf16[16,2048]{1,0:T(8,128)(2,1)} copy(bf16[16,2048]{1,0:T(8,128)(2,1)} %cascade.1) | data formatting | bytes 131072

commit v2 on v1

--- a/solution.py
+++ b/solution.py
@@ -28,7 +28,7 @@
 def kernel(
     n, rows, tokens, groups, tb,
     q_ref, rb_ref, len_ref, rk_ref, rv_ref, bk_ref, bv_ref, out_ref,
-    qall, kbuf, vbuf, qbr, sbuf, mbuf, acc, rnum, rm, spread_e,
+    qall, kbuf, vbuf, sbuf, mbuf, acc, rnum, rm, right, spread_e,
     send_o, send_l, recv_o, recv_l,
     kv_sem, q_own, q_send, q_recv, o_send, o_recv, l_send, l_recv,
 ):
@@ -50,8 +50,7 @@
     ]
     own = pltpu.make_async_copy(q_ref, qall.at[me], q_own)
     own.start()
-    for copy in copies:
-        copy.start()
+    copies[2].start()
 
     barrier = pltpu.get_barrier_semaphore()
     for off in range(1, n):
@@ -59,15 +58,19 @@
         pl.semaphore_signal(barrier, inc=1, device_id={"branch": peer}, device_id_type=MESH)
     pl.semaphore_wait(barrier, n - 1)
 
-    q_copies = []
-    for off in range(1, n):
-        peer = me ^ off
-        copy = pltpu.make_async_remote_copy(
-            src_ref=q_ref, dst_ref=qall.at[me], send_sem=q_send.at[off],
-            recv_sem=q_recv.at[off], device_id={"branch": peer}, device_id_type=MESH,
-        )
-        copy.start()
-        q_copies.append(copy)
+    q_copies = {}
+    for g in range(groups):
+        for off in range(1, n):
+            peer = me ^ off
+            cols = pl.ds(g * PER * HD, PER * HD)
+            copy = pltpu.make_async_remote_copy(
+                src_ref=q_ref.at[:, cols], dst_ref=qall.at[me, :, cols],
+                send_sem=q_send.at[g, off], recv_sem=q_recv.at[g, off],
+                device_id={"branch": peer}, device_id_type=MESH,
+            )
+            copy.start()
+            q_copies[g, off] = copy
+    copies[3].start()
 
     rb = rb_ref[...]
     mem_row = jnp.where(rb == me, 1.0, 0.0).astype(F32)
@@ -91,55 +94,57 @@
     spread_e[...] = e_full
     length = len_ref[0]
 
-    def stack(q, g):
-        return jnp.concatenate(
-            [q[:, (g * PER + p) * HD:(g * PER + p + 1) * HD] for p in range(PER)], axis=0
-        )
-
-    def chunk_of(k):
-        return lax.rem(me // 2 + k, chunks)
+    def stack(q):
+        return jnp.concatenate([q[:, p * HD:(p + 1) * HD] for p in range(PER)], axis=0)
 
     tasks = []
     for g in range(groups):
-        tasks.append((0, g, 0))
-    for g in range(groups):
-        for k in range(1, chunks):
-            tasks.append((0, g, k))
-        tasks.append((1, g, 0))
+        tasks += [(1, g, 0)] + [(0, g, k) for k in range(1, chunks)]
+    tasks += [(0, g, 0) for g in range(groups)]
 
     waited = set()
+    started = {2, 3}
 
     def need(index):
         if index not in waited:
             waited.add(index)
             copies[index].wait()
 
-    def need_q(off):
-        key = ("q", off)
+    def launch(index):
+        if index not in started:
+            started.add(index)
+            copies[index].start()
+
+    def need_q(g, off):
+        key = ("q", g, off)
         if key not in waited:
             waited.add(key)
-            if off == 0:
+            if off > 0:
+                q_copies[g, off].wait_recv()
+            elif ("own",) not in waited:
+                waited.add(("own",))
                 own.wait()
-            else:
-                q_copies[off - 1].wait_recv()
 
     def stage(first, second, slot):
         if first is not None:
             src, g, k = first
+            cols = slice(g * PER * HD, (g + 1) * PER * HD)
+            launch(2 * src)
             need(2 * src)
+            launch(2 * src + 1)
+            launch(0)
+            if second is not None:
+                launch(1)
             if src == 0:
-                need_q(2 * k)
-                need_q(2 * k + 1)
+                need_q(g, 2 * k)
+                need_q(g, 2 * k + 1)
                 base = (me // 2) ^ k
-                q_here = qall[pl.ds(base * 2, 2)].reshape(slots, groups * PER * HD)
-                query = stack(q_here, g)
+                query = stack(qall[pl.ds(base * 2, 2), :, cols].reshape(slots, PER * HD))
             else:
                 for off in range(n):
-                    need_q(off)
-                if g == 0:
-                    whole = qall[...].reshape(all_rows, groups * PER * HD)
-                    qbr[...] = jnp.dot(picker, whole, preferred_element_type=F32).astype(BF)
-                query = stack(qbr[...], g)
+                    need_q(g, off)
+                whole = qall[:, :, cols].reshape(all_rows, PER * HD)
+                query = stack(jnp.dot(picker, whole, preferred_element_type=F32).astype(BF))
             mbuf[slot] = jnp.full((m_rows, HD), NEG, F32)
         if second is not None:
             src2, g2, k2 = second
@@ -178,6 +183,15 @@
         if second is not None and src2 == 0:
             rnum[g2, k2] = acc[...]
             rm[g2, k2] = mbuf[other]
+        elif second is not None:
+            numer, total, top = acc[:, :HD], acc[:, HD:], mbuf[other]
+            for p in range(PER):
+                lo, hi = p * slots, (p + 1) * slots
+                gap = [jnp.zeros((slots, HD), BF)]
+                pieces = (split(numer[lo:hi], 2) + gap, split(total[lo:hi], 2) + gap, split(top[lo:hi], 3))
+                right[g2, p] = jnp.concatenate(
+                    [jnp.concatenate(piece, axis=0) for piece in pieces], axis=1
+                )
 
     eye = (
         lax.broadcasted_iota(jnp.int32, (part, part), 0)
@@ -185,47 +199,35 @@
     )
     sent = []
 
-    def finish(g, other):
-        numer = acc[:, :HD]
-        total = acc[:, HD:]
-        top = mbuf[other]
-        rights = []
+    def finish(g, k):
+        base = (me // 2) ^ k
+        e = spread_e[pl.ds(pl.multiple_of(base * slots, slots), slots), :]
+        e3 = jnp.concatenate([e, e, e], axis=1)
+        has = jnp.sum(e.astype(F32), axis=1, keepdims=True) > 0.5
+        has = jnp.broadcast_to(has, (slots, HD))
+        whole_o, whole_l = [], []
         for p in range(PER):
             lo, hi = p * slots, (p + 1) * slots
-            a = jnp.concatenate(split(numer[lo:hi], 2) + [jnp.zeros((slots, HD), BF)], axis=0)
-            b = jnp.concatenate(split(total[lo:hi], 2) + [jnp.zeros((slots, HD), BF)], axis=0)
-            c = jnp.concatenate(split(top[lo:hi], 3), axis=0)
-            rights.append(jnp.concatenate([a, b, c], axis=1))
-        for k in range(chunks):
-            base = (me // 2) ^ k
-            e = spread_e[pl.ds(pl.multiple_of(base * slots, slots), slots), :]
-            e3 = jnp.concatenate([e, e, e], axis=1)
-            has = jnp.sum(e.astype(F32), axis=1, keepdims=True) > 0.5
-            has = jnp.broadcast_to(has, (slots, HD))
-            whole_o, whole_l = [], []
-            for p in range(PER):
-                lo, hi = p * slots, (p + 1) * slots
-                back = jnp.dot(e3, rights[p], preferred_element_type=F32)
-                r_num = rnum[g, k, lo:hi, :HD]
-                r_tot = rnum[g, k, lo:hi, HD:]
-                r_top = rm[g, k, lo:hi]
-                b_top = jnp.where(has, back[:, 2 * HD:], NEG)
-                peak = jnp.maximum(r_top, b_top)
-                x = jnp.exp2(r_top - peak)
-                y = jnp.exp2(b_top - peak)
-                num = r_num * x + back[:, :HD] * y
-                tot = r_tot * x + back[:, HD:2 * HD] * y
-                whole_o.append((num / tot).astype(BF))
-                whole_l.append(peak + jnp.log2(tot))
-            for half in range(2):
-                off_slot = 2 * k + half
-                lo, hi = half * rows, (half + 1) * rows
-                send_o[g, off_slot] = jnp.concatenate([o[lo:hi] for o in whole_o], axis=0)
-                lse = jnp.concatenate([v[lo:hi] for v in whole_l], axis=0)
-                line = jnp.sum(jnp.where(eye, lse, 0.0), axis=0, keepdims=True)
-                send_l[g, off_slot] = jnp.broadcast_to(line, (8, part))
-        for off in range(1, n):
-            k = off // 2
+            back = jnp.dot(e3, right[g, p], preferred_element_type=F32)
+            r_num = rnum[g, k, lo:hi, :HD]
+            r_tot = rnum[g, k, lo:hi, HD:]
+            r_top = rm[g, k, lo:hi]
+            b_top = jnp.where(has, back[:, 2 * HD:], NEG)
+            peak = jnp.maximum(r_top, b_top)
+            x = jnp.exp2(r_top - peak)
+            y = jnp.exp2(b_top - peak)
+            num = r_num * x + back[:, :HD] * y
+            tot = r_tot * x + back[:, HD:2 * HD] * y
+            whole_o.append((num / tot).astype(BF))
+            whole_l.append(peak + jnp.log2(tot))
+        for half in range(2):
+            off_slot = 2 * k + half
+            lo, hi = half * rows, (half + 1) * rows
+            send_o[g, off_slot] = jnp.concatenate([o[lo:hi] for o in whole_o], axis=0)
+            lse = jnp.concatenate([v[lo:hi] for v in whole_l], axis=0)
+            line = jnp.sum(jnp.where(eye, lse, 0.0), axis=0, keepdims=True)
+            send_l[g, off_slot] = jnp.broadcast_to(line, (8, part))
+        for off in range(max(1, 2 * k), 2 * k + 2):
             peer = me ^ off
             index = 2 * k + lax.rem(peer, 2)
             pair = []
@@ -264,14 +266,20 @@
             out_ref[:, (g * PER + p) * HD:(g * PER + p + 1) * HD] = result[p * rows:(p + 1) * rows]
 
     previous = None
+    done, finished = set(), set()
     for t, task in enumerate(tasks + [None]):
         stage(task, previous, t % 2)
-        if previous is not None and previous[0] == 1:
-            finish(previous[1], 1 - t % 2)
+        if previous is not None:
+            done.add(previous)
+            for g in range(groups):
+                for k in reversed(range(chunks)):
+                    if (1, g, 0) in done and (0, g, k) in done and (g, k) not in finished:
+                        finished.add((g, k))
+                        finish(g, k)
         previous = task
     for g in range(groups):
         collect(g)
-    for copy in q_copies:
+    for copy in q_copies.values():
         copy.wait_send()
     for _, _, pair in sent:
         for copy in pair:
@@ -290,7 +298,7 @@
     slots = 2 * rows
     m_rows = slots * PER
     part = rows * PER
-    tb = min(1024, tokens)
+    tb = min(2048, tokens)
     vmem = pl.BlockSpec(memory_space=pltpu.VMEM)
     smem = pl.BlockSpec(memory_space=pltpu.SMEM)
     hbm = pl.BlockSpec(memory_space=pl.ANY)
@@ -304,18 +312,18 @@
             pltpu.VMEM((n, rows, groups * PER * HD), BF),
             pltpu.VMEM((2, tokens, width), BF),
             pltpu.VMEM((2, tokens, width), BF),
-            pltpu.VMEM((slots, groups * PER * HD), BF),
             pltpu.VMEM((2, tokens // tb, m_rows, tb), F32),
             pltpu.VMEM((2, m_rows, HD), F32),
             pltpu.VMEM((m_rows, 2 * HD), F32),
             pltpu.VMEM((groups, chunks, m_rows, 2 * HD), F32),
             pltpu.VMEM((groups, chunks, m_rows, HD), F32),
+            pltpu.VMEM((groups, PER, 3 * slots, 3 * HD), BF),
             pltpu.VMEM((all_rows, slots), BF),
             pltpu.VMEM((groups, n, part, HD), BF),
             pltpu.VMEM((groups, n, 8, part), F32),
             pltpu.VMEM((groups, n, part, HD), BF),
             pltpu.VMEM((groups, n, 8, part), F32),
-            dma((4,)), dma, dma((n,)), dma((n,)),
+            dma((4,)), dma, dma((groups, n)), dma((groups, n)),
             dma((groups, n)), dma((groups, n)), dma((groups, n)), dma((groups, n)),
         ],
         compiler_params=pltpu.CompilerParams(

time: 25.3 us -> 23.2 us (0.917)
  Pallas kernels: 22.9 us -> 20.8 us
    pallas_call x1, Pallas kernels: 22.9 us -> 20.8 us  [on_device(): pl.pallas_call(functools.partial(kernel, n, rows, tokens, groups, tb), ou...]
where the time goes in v2:
time: 23.2 us; the launch traced here: 22.9 us
  Pallas kernels  20.8 us (90%)
  local copies, waits for them, and re-layouts  1.47 us (6%)
  between operations  0.66 us (3%)
    pallas_call x1, Pallas kernels, on_device(): pl.pallas_call(functools.partial(kernel, n, rows, tokens, groups, tb), ou...  20.8 us
    unnamed x1, local copies, waits for them, and re-layouts  1.47 us

profile of v2, /device:TPU:0, one launch (start us, length us, event | category | flops | bytes accessed | tf_op | source)
XLA Modules:
  0.0 22.9 jit_solution(6960158514949527829)
XLA Ops:
  0.7 20.8 %cascade.1 = bf16[16,2048]{1,0:T(8,128)(2,1)} custom-call(bf16[16,2048]{1,0:T(8,128)(2,1)} %q_ref.1, s32[1,64]{1,0:T(1,128)} %bitcast.1, s32[1]{0:T(128)S(6)} %copy.9.len_ref, bf16[4096,256]{1,0:T(8,128)(2,1)} %rk_ref.1, bf16[4096,256]{1,0:T(8,128)(2,1)} %rv_ref.1, bf16[1,4096,256]{2,1,0:T(8,128)(2,1)} %bk_ref.1, bf16[1,4096,256]{2,1,0:T(8,128)(2,1)} %bv_ref.1), custom_call_target="tpu_custom_call" | custom-call | tf_op jit(solution)/shard_map/cascade/pallas_call | solution.py:306
  21.5 1.5 %copy.10 = bf16[16,2048]{1,0:T(8,128)(2,1)} copy(bf16[16,2048]{1,0:T(8,128)(2,1)} %cascade.1) | data formatting | bytes 131072

commit v3 on v2

--- a/solution.py
+++ b/solution.py
@@ -60,7 +60,7 @@
 
     q_copies = {}
     for g in range(groups):
-        for off in range(1, n):
+        for off in reversed(range(1, n)):
             peer = me ^ off
             cols = pl.ds(g * PER * HD, PER * HD)
             copy = pltpu.make_async_remote_copy(

time: 23.2 us -> 22.7 us (0.978)
  Pallas kernels: 20.8 us -> 20.3 us
    pallas_call x1, Pallas kernels: 20.8 us -> 20.3 us  [on_device(): pl.pallas_call(functools.partial(kernel, n, rows, tokens, groups, tb), ou...]
where the time goes in v3:
time: 22.7 us; the launch traced here: 22.5 us
  Pallas kernels  20.3 us (89%)
  local copies, waits for them, and re-layouts  1.47 us (6%)
  between operations  0.66 us (3%)
    pallas_call x1, Pallas kernels, on_device(): pl.pallas_call(functools.partial(kernel, n, rows, tokens, groups, tb), ou...  20.3 us
    unnamed x1, local copies, waits for them, and re-layouts  1.47 us

profile of v3, /device:TPU:0, one launch (start us, length us, event | category | flops | bytes accessed | tf_op | source)
XLA Modules:
  0.0 22.5 jit_solution(15700531777459688362)
XLA Ops:
  0.7 20.3 %cascade.1 = bf16[16,2048]{1,0:T(8,128)(2,1)} custom-call(bf16[16,2048]{1,0:T(8,128)(2,1)} %q_ref.1, s32[1,64]{1,0:T(1,128)} %bitcast.1, s32[1]{0:T(128)S(6)} %copy.9.len_ref, bf16[4096,256]{1,0:T(8,128)(2,1)} %rk_ref.1, bf16[4096,256]{1,0:T(8,128)(2,1)} %rv_ref.1, bf16[1,4096,256]{2,1,0:T(8,128)(2,1)} %bk_ref.1, bf16[1,4096,256]{2,1,0:T(8,128)(2,1)} %bv_ref.1), custom_call_target="tpu_custom_call" | custom-call | tf_op jit(solution)/shard_map/cascade/pallas_call | solution.py:306
  21.0 1.5 %copy.10 = bf16[16,2048]{1,0:T(8,128)(2,1)} copy(bf16[16,2048]{1,0:T(8,128)(2,1)} %cascade.1) | data formatting | bytes 131072
